TPU v7x, 32 devices: a whole 2x2x4 slice. The times are simulated.
32 devices in a mesh: groups: 2 (over y), feat: 8 (over z, x), corp: 2 (over core).
Axes of the slice: x: 2, y: 2, z: 4, core: 2. Of those that a mesh axis runs over, the one named last changes fastest.
Arguments:
- query_features: bfloat16 [1536, 16384], P(('groups', 'corp'), 'feat'), parts along dimension 0, may hold values from -6 to 6
- inverse_kernel: bfloat16 [16384, 16384], P(None, 'feat'), may hold values from -1 to 3, as said below
- doc_features: bfloat16 [512, 16384], P(('groups', 'corp'), 'feat'), parts along dimension 0, may hold values from -0.046875 to 0.046875
Outputs:
- scores: float32 [1536, 256], P(('groups', 'feat'), 'corp'), parts along dimension 0
There are 2 independent parts, one for each index of `groups`. A program takes and returns all parts, laid end to end along the dimension named above; an argument that names none is the same for every part. Nothing has to cross between parts.
Inputs may be any that keep to these rules, and one draw needn't show every extreme that they name: inverse_kernel is symmetric.
All inputs are finite; a program needn't handle non-finite values.
Results may differ from a plain program's by a relative error of at most 0.0003.
Values may be sent and summed in bfloat16 or wider, within the bound.
No kernel may reach another device: no remote copies, remote signals or barrier semaphores. Data moves between devices by JAX's collectives and lax.ppermute only.
A program may use at most 128 MiB of HBM per device.

v0:
```python
import jax
import jax.numpy as jnp
from jax import lax
from jax.sharding import PartitionSpec as P


def on_device(query_features, inverse_kernel, doc_features):
    applied = jnp.dot(
        lax.all_gather(doc_features, "feat", axis=1, tiled=True),
        inverse_kernel,
        preferred_element_type=jnp.float32,
    )
    left_rows = lax.all_gather(query_features, "corp", axis=0, tiled=True).astype(jnp.float32)
    return lax.psum_scatter(
        lax.dot_general(
            left_rows,
            applied,
            (((1,), (1,)), ((), ())),
            precision=lax.Precision.HIGHEST,
            preferred_element_type=jnp.float32,
        ),
        "feat",
        scatter_dimension=0,
        tiled=True,
    )


def solution(mesh):
    placed = (P(("groups", "corp"), "feat"), P(None, "feat"), P(("groups", "corp"), "feat"))
    return jax.shard_map(
        on_device,
        mesh=mesh,
        in_specs=placed,
        out_specs=P(("groups", "feat"), "corp"),
        check_vma=False,
    )
```

profile of v0, /device:TPU:0, one launch (start us, length us, event | category | flops | bytes accessed | tf_op | source)
XLA Modules:
  0.0 184.1 jit_solution(11617538823632090180)
XLA Ops:
  6.5 0.0 all-gather.3.cloned.1.call-start
  6.5 0.7 all-gather.3.cloned.1.call-update
  7.3 0.0 all-gather.5.cloned.1.call-start
  7.3 0.7 all-gather.5.cloned.1.call-update
  8.0 0.0 reduce-scatter.4.cloned.1.call-start
  8.1 77.0 %all-gather.3.cloned.1.call-done = bf16[128,16384]{1,0:T(8,128)(2,1)} async-done(((bf16[128,2048]{1,0:T(8,128)(2,1)}), bf16[128,16384]{1,0:T(8,128)(2,1)}) %all-gather.3.cloned.1.call-update) | async-done | bytes 4194320 | tf_op jit(solution)/shard_map/all_gather | solution.py:9
  85.0 25.5 %fusion = f32[128,2048]{1,0:T(8,128)S(1)} fusion(bf16[128,16384]{1,0:T(8,128)(2,1)} %all-gather.3.cloned.1.call-done, bf16[16384,2048]{1,0:T(8,128)(2,1)} %param.4), kind=kOutput, calls=%fused_computation.1 | convolution fusion | flops 8589934592 | bytes 72351744 | tf_op jit(solution)/shard_map/dot_general | solution.py:8
  110.6 0.0 all-gather.5.cloned.1.call-done
  110.6 5.1 %convolution_bitcast_fusion = f32[768,128]{0,1:T(8,128)S(1)} fusion(f32[128,2048]{1,0:T(8,128)S(1)} %fusion, bf16[768,2048]{1,0:T(8,128)(2,1)} %all-gather.5.cloned.1.call-done), kind=kOutput, calls=%fused_computation | convolution fusion | flops 2415919104 | bytes 4587520 | tf_op jit(solution)/shard_map/dot_general | solution.py:15
  115.7 0.9 copy.6
  116.6 0.0 reduce-scatter.4.cloned.1.call-update
  116.6 60.9 %reduce-scatter.4.cloned.1.call-done = f32[96,128]{1,0:T(8,128)} async-done(((f32[768,128]{1,0:T(8,128)}), f32[96,128]{1,0:T(8,128)}) %reduce-scatter.4.cloned.1.call-update) | async-done | bytes 49168 | tf_op jit(solution)/shard_map/reduce_scatter | solution.py:14
Async XLA Ops:
  6.5 78.5 %all-gather.3.cloned.1.call-start = ((), (), s32[]{:S(2)}) async-start(), calls=%async_computation.1 | async-start | bytes 4718592 | tf_op jit(solution)/shard_map/all_gather | solution.py:9
  7.3 103.3 %all-gather.5.cloned.1.call-start = ((), (), s32[]{:S(2)}) async-start(), calls=%async_computation.2 | async-start | bytes 4718592 | tf_op jit(solution)/shard_map/all_gather | solution.py:13
  8.0 169.6 %reduce-scatter.4.cloned.1.call-start = ((), (), s32[]{:S(2)}) async-start(), calls=%async_computation.3 | async-start | bytes 442368 | tf_op jit(solution)/shard_map/reduce_scatter | solution.py:14
Sparse Core Ops, SparseCore 0:
  9.5 75.4 all-gather.2
  86.6 10.6 all-gather.4
  116.7 60.7 reduce-scatter.3
where the time goes:
time: 184 us
  waiting for transfers between devices  139 us (76%)
  matrix products  30.6 us (17%)
  between operations  13.1 us (7%)
    all_gather x1, waiting for transfers between devices, on_device(): lax.all_gather(doc_features, 'feat', axis=1, tiled=True)  77 us
    reduce_scatter x1, waiting for transfers between devices, on_device(): lax.psum_scatter(lax.dot_general(left_rows, applied, (((1,), (1,)), ((),...  60.9 us
    dot_general x1, matrix products, on_device(): jnp.dot(lax.all_gather(doc_features, 'feat', axis=1, tiled=True), inverse...  25.5 us
    dot_general x1, matrix products, on_device(): lax.dot_general(left_rows, applied, (((1,), (1,)), ((), ())), precision=l...  5.07 us
  transfers between devices with their start and end apart: 3, of which 2 were waited for; matrix products, arithmetic and copies ran while one was open for 14% of the time, Pallas kernels for 0%

commit v1 on v0

--- a/solution.py
+++ b/solution.py
@@ -4,11 +4,31 @@
 from jax.sharding import PartitionSpec as P
 
 
+def joined_along(parts, dim):
+    lengths = list(parts.shape[1:])
+    lengths[dim] *= parts.shape[0]
+    return jnp.moveaxis(parts, 0, dim).reshape(lengths)
+
+
+def collected_by_bits(x, axis):
+    size = lax.axis_size(axis)
+    pieces = x[None]
+    for level in range(size.bit_length() - 1):
+        stride = 1 << level
+        other = lax.ppermute(pieces, axis, [(i, i ^ stride) for i in range(size)])
+        both = jnp.stack([pieces, other])
+        upper = lax.axis_index(axis) >> level & 1
+        pieces = jnp.where(upper == 0, both, both[::-1]).reshape(-1, *x.shape)
+    return pieces
+
+
+def gather_by_bits(x, axis, dim):
+    return joined_along(collected_by_bits(x, axis), dim)
+
+
 def on_device(query_features, inverse_kernel, doc_features):
     applied = jnp.dot(
-        lax.all_gather(doc_features, "feat", axis=1, tiled=True),
-        inverse_kernel,
-        preferred_element_type=jnp.float32,
+        gather_by_bits(doc_features, "feat", 1), inverse_kernel, preferred_element_type=jnp.float32
     )
     left_rows = lax.all_gather(query_features, "corp", axis=0, tiled=True).astype(jnp.float32)
     return lax.psum_scatter(

time: 184 us -> 249 us (1.35)
  waiting for transfers between devices: 139 us -> 185 us
  other arithmetic: 0 us -> 7.58 us
  starting transfers between devices: 0.08 us -> 7.47 us
  local copies, waits for them, and re-layouts: 0.93 us -> 5.94 us
    ppermute x0 -> x3, waiting for transfers between devices: none -> 122 us  [collected_by_bits(): other = lax.ppermute(pieces, axis, [(i, i ^ stride) for i in range(size)])]
    all_gather x1 -> x0, waiting for transfers between devices: 77 us -> none  [on_device(): lax.all_gather(doc_features, 'feat', axis=1, tiled=True)]
    ppermute x0 -> x3, starting transfers between devices: none -> 7.42 us  [collected_by_bits(): other = lax.ppermute(pieces, axis, [(i, i ^ stride) for i in range(size)])]
    another operation x0 -> x4, other arithmetic: none -> 4.35 us  [collected_by_bits(): both = jnp.stack([pieces, other])]
    select_n x0 -> x2, other arithmetic: none -> 3.23 us  [collected_by_bits(): pieces = jnp.where(upper == 0, both, both[::-1]).reshape(-1, *x.shape)]
    another operation x0 -> x1, local copies, waits for them, and re-layouts: none -> 2.52 us  [collected_by_bits(): both = jnp.stack([pieces, other])]
    reshape x0 -> x1, local copies, waits for them, and re-layouts: none -> 2.5 us  [collected_by_bits(): pieces = jnp.where(upper == 0, both, both[::-1]).reshape(-1, *x.shape)]
  transfers between devices with their start and end apart: 3 -> 5, of which waited for: 2 -> 4; matrix products, arithmetic and copies ran while one was open for 14% -> 13% of each run, Pallas kernels for 0% -> 0%
where the time goes in v1:
time: 249 us; the launch traced here: 248 us
  waiting for transfers between devices  185 us (74%)
  matrix products  29.1 us (12%)
  between operations  13.5 us (5%)
  other arithmetic  7.58 us (3%)
  starting transfers between devices  7.47 us (3%)
  local copies, waits for them, and re-layouts  5.94 us (2%)
    ppermute x3, waiting for transfers between devices, collected_by_bits(): other = lax.ppermute(pieces, axis, [(i, i ^ stride) for i in range(size)])  122 us
    reduce_scatter x1, waiting for transfers between devices, on_device(): lax.psum_scatter(lax.dot_general(left_rows, applied, (((1,), (1,)), ((),...  63.2 us
    dot_general x1, matrix products, on_device(): jnp.dot(gather_by_bits(doc_features, 'feat', 1), inverse_kernel, preferre...  24 us
    ppermute x3, starting transfers between devices, collected_by_bits(): other = lax.ppermute(pieces, axis, [(i, i ^ stride) for i in range(size)])  7.42 us
    dot_general x1, matrix products, on_device(): lax.dot_general(left_rows, applied, (((1,), (1,)), ((), ())), precision=l...  5.07 us
  transfers between devices with their start and end apart: 5, of which 4 were waited for; matrix products, arithmetic and copies ran while one was open for 13% of the time, Pallas kernels for 0%

profile of v1, /device:TPU:0, one launch (start us, length us, event | category | flops | bytes accessed | tf_op | source)
XLA Modules:
  0.0 248.3 jit_solution(10318114795731122448)
XLA Ops:
  6.5 0.0 all-gather.2.cloned.1.call-start
  6.5 3.0 %collective-permute-start = (bf16[1,128,2048]{2,1,0:T(8,128)(2,1)}, bf16[1,128,2048]{2,1,0:T(8,128)(2,1)S(1)}, u32[]{:S(2)}, u32[]{:S(2)}) collective-permute-start(bf16[1,128,2048]{2,1,0:T(8,128)(2,1)} %bitcast.27), channel_id=1, source_target_pairs={{0,2},{2,0},{4,6},{6,4},{8,10},{10,8},{12,14},{14,12},{1,3},{3,1},... | collective-permute-start | bytes 1572872 | tf_op jit(solution)/shard_map/ppermute | solution.py:18
  9.5 12.1 %collective-permute-done = bf16[1,128,2048]{2,1,0:T(8,128)(2,1)S(1)} collective-permute-done((bf16[1,128,2048]{2,1,0:T(8,128)(2,1)}, bf16[1,128,2048]{2,1,0:T(8,128)(2,1)S(1)}, u32[]{:S(2)}, u32[]{:S(2)}) %collective-permute-start) | collective-permute-done | bytes 524320 | tf_op jit(solution)/shard_map/ppermute | solution.py:18
  21.6 1.1 pad_maximum_fusion.2
  22.8 0.4 fusion.1
  23.2 1.9 collective-permute-start.1
  25.1 22.5 %collective-permute-done.1 = bf16[2,128,2048]{2,1,0:T(8,128)(2,1)S(1)} collective-permute-done((bf16[2,128,2048]{2,1,0:T(8,128)(2,1)S(1)}, bf16[2,128,2048]{2,1,0:T(8,128)(2,1)S(1)}, u32[]{:S(2)}, u32[]{:S(2)}) %collective-permute-start.1) | collective-permute-done | bytes 1048608 | tf_op jit(solution)/shard_map/ppermute | solution.py:18
  47.6 0.2 pad_maximum_fusion.1
  47.8 0.5 reverse_select_fusion.1
  48.3 2.5 %copy.8 = bf16[4,128,2048]{1,2,0:T(8,128)(2,1)} copy(bf16[4,128,2048]{2,1,0:T(8,128)(2,1)S(1)} %bitcast.23) | data formatting | bytes 4194304 | tf_op jit(solution)/shard_map/reshape | solution.py:21
  50.8 2.6 %collective-permute-start.2 = (bf16[4,128,2048]{1,2,0:T(8,128)(2,1)}, bf16[4,128,2048]{1,2,0:T(8,128)(2,1)}, u32[]{:S(2)}, u32[]{:S(2)}) collective-permute-start(bf16[4,128,2048]{1,2,0:T(8,128)(2,1)} %copy.8), channel_id=1, source_target_pairs={{0,8},{2,10},{4,12},{6,14},{8,0},{10,2},{12,4},{14,6},{1,9},{3,11}... | collective-permute-start | bytes 6291464 | tf_op jit(solution)/shard_map/ppermute | solution.py:18
  53.3 0.0 all-gather.2.cloned.1.call-update
  53.4 0.0 reduce-scatter.4.cloned.1.call-start
  53.4 2.5 %copy.9 = bf16[1,4,128,2048]{2,3,1,0:T(8,128)(2,1)} copy(bf16[1,4,128,2048]{3,2,1,0:T(8,128)(2,1)S(1)} %bitcast.24) | data formatting | bytes 4194304 | tf_op jit(solution)/shard_map/stack;reshape | solution.py:19
  55.9 86.9 %collective-permute-done.2 = bf16[4,128,2048]{1,2,0:T(8,128)(2,1)} collective-permute-done((bf16[4,128,2048]{1,2,0:T(8,128)(2,1)}, bf16[4,128,2048]{1,2,0:T(8,128)(2,1)}, u32[]{:S(2)}, u32[]{:S(2)}) %collective-permute-start.2) | collective-permute-done | bytes 2097184 | tf_op jit(solution)/shard_map/ppermute | solution.py:18
  142.9 2.6 %pad_maximum_fusion = bf16[2,4,128,2048]{2,3,1,0:T(8,128)(2,1)S(1)} fusion(bf16[1,4,128,2048]{2,3,1,0:T(8,128)(2,1)} %bitcast.8, bf16[1,4,128,2048]{2,3,1,0:T(8,128)(2,1)} %copy.9), kind=kLoop, calls=%fused_computation.1 | loop fusion | flops 2097152 | bytes 8388608 | tf_op jit(solution)/shard_map/stack | solution.py:19
  145.5 2.8 %reverse_select_fusion = bf16[2,4,128,2048]{2,3,1,0:T(8,128)(2,1)} fusion(bf16[2,4,128,2048]{2,3,1,0:T(8,128)(2,1)S(1)} %pad_maximum_fusion, pred[]{:T(512)S(6)} %eq.9), kind=kLoop, calls=%fused_computation | loop fusion | flops 2097152 | bytes 8388609 | tf_op jit(solution)/shard_map/jit(_where)/select_n | solution.py:21
  148.2 24.0 %fusion.2 = f32[128,2048]{1,0:T(8,128)S(1)} fusion(bf16[128,16384]{0,1:T(8,128)(2,1)} %bitcast.25, bf16[16384,2048]{1,0:T(8,128)(2,1)} %param.4), kind=kOutput, calls=%fused_computation.9 | convolution fusion | flops 8589934592 | bytes 72351744 | tf_op jit(solution)/shard_map/dot_general | solution.py:30
  172.2 0.0 all-gather.2.cloned.1.call-done
  172.3 5.1 %convolution_bitcast_fusion = f32[768,128]{0,1:T(8,128)S(1)} fusion(f32[128,2048]{1,0:T(8,128)S(1)} %fusion.2, bf16[768,2048]{1,0:T(8,128)(2,1)} %all-gather.2.cloned.1.call-done), kind=kOutput, calls=%fused_computation.5 | convolution fusion | flops 2415919104 | bytes 4587520 | tf_op jit(solution)/shard_map/dot_general | solution.py:35
  177.3 0.9 copy.11
  178.2 0.0 reduce-scatter.4.cloned.1.call-update
  178.3 63.2 %reduce-scatter.4.cloned.1.call-done = f32[96,128]{1,0:T(8,128)} async-done(((f32[768,128]{1,0:T(8,128)}), f32[96,128]{1,0:T(8,128)}) %reduce-scatter.4.cloned.1.call-update) | async-done | bytes 49168 | tf_op jit(solution)/shard_map/reduce_scatter | solution.py:34
Async XLA Ops:
  6.5 165.7 %all-gather.2.cloned.1.call-start = ((), (), s32[]{:S(2)}) async-start(), calls=%async_computation.1 | async-start | bytes 4718592 | tf_op jit(solution)/shard_map/all_gather | solution.py:33
  6.5 15.1 %collective-permute-start = (bf16[1,128,2048]{2,1,0:T(8,128)(2,1)}, bf16[1,128,2048]{2,1,0:T(8,128)(2,1)S(1)}, u32[]{:S(2)}, u32[]{:S(2)}) collective-permute-start(bf16[1,128,2048]{2,1,0:T(8,128)(2,1)} %bitcast.27), channel_id=1, source_target_pairs={{0,2},{2,0},{4,6},{6,4},{8,10},{10,8},{12,14},{14,12},{1,3},{3,1},... | collective-permute-start | bytes 1572872 | tf_op jit(solution)/shard_map/ppermute | solution.py:18
  23.2 24.4 %collective-permute-start.1 = (bf16[2,128,2048]{2,1,0:T(8,128)(2,1)S(1)}, bf16[2,128,2048]{2,1,0:T(8,128)(2,1)S(1)}, u32[]{:S(2)}, u32[]{:S(2)}) collective-permute-start(bf16[2,128,2048]{2,1,0:T(8,128)(2,1)S(1)} %get-tuple-element.6), channel_id=1, source_target_pairs={{0,4},{2,6},{4,0},{6,2},{8,12},{10,14},{12,8},{14,10},{1,5},{3,7},... | collective-permute-start | bytes 3145736 | tf_op jit(solution)/shard_map/ppermute | solution.py:18
  50.8 92.1 %collective-permute-start.2 = (bf16[4,128,2048]{1,2,0:T(8,128)(2,1)}, bf16[4,128,2048]{1,2,0:T(8,128)(2,1)}, u32[]{:S(2)}, u32[]{:S(2)}) collective-permute-start(bf16[4,128,2048]{1,2,0:T(8,128)(2,1)} %copy.8), channel_id=1, source_target_pairs={{0,8},{2,10},{4,12},{6,14},{8,0},{10,2},{12,4},{14,6},{1,9},{3,11}... | collective-permute-start | bytes 6291464 | tf_op jit(solution)/shard_map/ppermute | solution.py:18
  53.4 188.1 %reduce-scatter.4.cloned.1.call-start = ((), (), s32[]{:S(2)}) async-start(), calls=%async_computation.2 | async-start | bytes 442368 | tf_op jit(solution)/shard_map/reduce_scatter | solution.py:34
Sparse Core Ops, SparseCore 0:
  53.5 11.3 all-gather.1
  178.4 63.0 reduce-scatter.3
